TPU v7x, 32 devices: a whole 2x2x4 slice. The times are simulated.
32 devices in a mesh: fsdp: 4 (over z), ctx: 4 (over x, core), tp: 2 (over y).
Axes of the slice: x: 2, y: 2, z: 4, core: 2. Of those that a mesh axis runs over, the one named last changes fastest.
Arguments:
- x_in: bfloat16 [8, 1024, 2048], P(None, ('fsdp', 'ctx')), may hold values from -6 to 6
- cotangent: bfloat16 [8, 1024, 2048], P(None, ('fsdp', 'ctx')), may hold values from -6 to 6
- lengths: int32 [8], replicated, may hold values from 128 to 1024, as said below
- adapter_ids: int32 [8], replicated, may hold values from 0 to 7
- w_qkv: bfloat16 [3, 2048, 2048], P(None, 'fsdp', 'tp'), may hold values from -0.125 to 0.125
- w_out: bfloat16 [2048, 2048], P('tp', 'fsdp'), may hold values from -2 to 2
- w_up: bfloat16 [2048, 8192], P('fsdp', 'tp'), may hold values from -0.125 to 0.125
- w_down: bfloat16 [8192, 2048], P('tp', 'fsdp'), may hold values from -0.0625 to 0.0625
- ln_gain: float32 [2, 2048], replicated, may hold values from 0.1 to 1.9
- ln_bias: float32 [2, 2048], replicated, may hold values from -1.5 to 1.5
- a_qkv: bfloat16 [3, 2048, 128], replicated, may hold values from -0.125 to 0.125
- b_qkv: bfloat16 [3, 128, 2048], P(None, None, 'tp'), may hold values from -0.5 to 0.5
- a_out: bfloat16 [2048, 128], P('tp'), may hold values from -2 to 2
- b_out: bfloat16 [128, 2048], replicated, may hold values from -0.5 to 0.5
- a_up: bfloat16 [2048, 128], replicated, may hold values from -0.125 to 0.125
- b_up: bfloat16 [128, 8192], P(None, 'tp'), may hold values from -0.5 to 0.5
- a_down: bfloat16 [8192, 128], P('tp'), may hold values from -0.0625 to 0.0625
- b_down: bfloat16 [128, 2048], replicated, may hold values from -0.5 to 0.5
Outputs:
- activations: bfloat16 [8, 1024, 2048], P(None, ('fsdp', 'ctx'))
- input_grad: bfloat16 [8, 1024, 2048], P(None, ('fsdp', 'ctx'))
- grad_a_qkv: float32 [3, 2048, 128], replicated
- grad_b_qkv: float32 [3, 128, 2048], P(None, None, 'tp')
- grad_a_out: float32 [2048, 128], P('tp')
- grad_b_out: float32 [128, 2048], replicated
- grad_a_up: float32 [2048, 128], replicated
- grad_b_up: float32 [128, 8192], P(None, 'tp')
- grad_a_down: float32 [8192, 128], P('tp')
- grad_b_down: float32 [128, 2048], replicated
Inputs may be any that keep to these rules, and one draw needn't show every extreme that they name: `lengths`: each aligned block of 2 sequences holds at least one sequence of length 1024.
All inputs are finite; a program needn't handle non-finite values.
Results may differ from a plain program's by a relative error of at most 0.019.
Values may be sent and summed in bfloat16 or wider, within the bound.
A program may use at most 256 MiB of HBM per device.

v0:
```python
from functools import partial
import math
import jax
import jax.numpy as jnp
from jax import lax
from jax.sharding import PartitionSpec as P

HEAD_DIM = 128
RANK = 16
ADAPTERS = 8
NORM_EPS = 1e-06
GELU_COEF = 0.7978845608028654


def norm_rows(values, gain_row, shift_row):
    center = values - jnp.mean(values, axis=-1, keepdims=True)
    spread = jnp.mean(center * center, axis=-1, keepdims=True)
    return center * lax.rsqrt(spread + NORM_EPS) * gain_row + shift_row


def gelu_tanh(values):
    return (
        0.5 * values * (1.0 + jnp.tanh(GELU_COEF * (values + 0.044715 * values * values * values)))
    )


def product(left_side, right_side):
    return jnp.dot(left_side, right_side, preferred_element_type=jnp.float32)


def against(left_side, right_side):
    return lax.dot_general(
        left_side, right_side, (((1,), (1,)), ((), ())), preferred_element_type=jnp.float32
    )


def across(left_side, right_side):
    return lax.dot_general(
        left_side, right_side, (((0,), (0,)), ((), ())), preferred_element_type=jnp.float32
    )


def local(
    x_in,
    cotangent,
    lengths,
    adapter_ids,
    w_qkv,
    w_out,
    w_up,
    w_down,
    ln_gain,
    ln_bias,
    a_qkv,
    b_qkv,
    a_out,
    b_out,
    a_up,
    b_up,
    a_down,
    b_down,
):
    n_ctx = lax.axis_size("ctx")
    n_fsdp = lax.axis_size("fsdp")
    owner_index = lax.axis_index("fsdp")
    seq_total, piece_rows, model_width = x_in.shape
    per_dev = seq_total // n_fsdp
    local_len = n_fsdp * piece_rows
    dev_rows = per_dev * local_len
    key_count = n_ctx * local_len
    heads_width = w_qkv.shape[2]
    heads_here = heads_width // HEAD_DIM
    score_scale = 1.0 / math.sqrt(HEAD_DIM)
    dealt_x, dealt_cot = (
        lax.all_to_all(x_in, "fsdp", split_axis=0, concat_axis=1, tiled=True),
        lax.all_to_all(cotangent, "fsdp", split_axis=0, concat_axis=1, tiled=True),
    )
    x_rows = dealt_x.reshape(dev_rows, model_width)
    my_lengths = lax.dynamic_slice_in_dim(lengths, owner_index * per_dev, per_dev)
    my_ids = lax.dynamic_slice_in_dim(adapter_ids, owner_index * per_dev, per_dev)
    picked = (my_ids[:, None] == jnp.arange(ADAPTERS)[None, :]).astype(jnp.float32)
    pick_rows = jnp.repeat(jnp.repeat(picked, RANK, axis=1), local_len, axis=0)
    key_index = jnp.arange(key_count)
    ctx_block = key_index // local_len
    remain = key_index % local_len
    key_pos = (remain // piece_rows * n_ctx + ctx_block) * piece_rows + remain % piece_rows
    usable = key_pos[None, :] < my_lengths[:, None]
    qkv_full, out_full = (
        lax.all_gather(w_qkv, "fsdp", axis=1, tiled=True),
        lax.all_gather(w_out, "fsdp", axis=1, tiled=True),
    )
    adapt_qkv = [
        (product(x_rows, a_qkv[proj_index]) * pick_rows).astype(jnp.bfloat16)
        for proj_index in range(3)
    ]
    projected = [
        (product(x_rows, qkv_full[proj_index]) + product(adapt_qkv[proj_index], b_qkv[proj_index]))
        .astype(jnp.bfloat16)
        .reshape(per_dev, local_len, heads_width)
        for proj_index in range(3)
    ]
    queries_all = projected[0]
    keys_all, values_all = (
        lax.all_gather(projected[1], "ctx", axis=1, tiled=True),
        lax.all_gather(projected[2], "ctx", axis=1, tiled=True),
    )

    def score_block(query_heads, key_heads, usable_row):
        scores = (
            jnp.einsum("qhd,khd->hqk", query_heads, key_heads, preferred_element_type=jnp.float32)
            * score_scale
        )
        return jnp.where(usable_row[None, None, :], scores, -1e30)

    def attend(packed):
        queries, keys_seq, values_seq, usable_row = packed
        query_heads = queries.reshape(local_len, heads_here, HEAD_DIM)
        key_heads = keys_seq.reshape(key_count, heads_here, HEAD_DIM)
        value_heads = values_seq.reshape(key_count, heads_here, HEAD_DIM)
        scores = score_block(query_heads, key_heads, usable_row)
        row_max = jnp.max(scores, axis=-1, keepdims=True)
        row_total = jnp.sum(jnp.exp(scores - row_max), axis=-1, keepdims=True)
        log_total = row_max + jnp.log(row_total)
        attn_probs = jnp.exp(scores - log_total).astype(jnp.bfloat16)
        mixed_heads = jnp.einsum(
            "hqk,khd->qhd", attn_probs, value_heads, preferred_element_type=jnp.float32
        )
        return (mixed_heads.reshape(local_len, heads_width).astype(jnp.bfloat16), log_total[..., 0])

    context, log_totals = lax.map(attend, (queries_all, keys_all, values_all, usable))
    ctx_rows = context.reshape(dev_rows, heads_width)
    part_out = product(ctx_rows, out_full)
    part_adapt = product(ctx_rows, a_out) * pick_rows
    attn_sum, adapt_out_sum = lax.psum((part_out, part_adapt), "tp")
    adapt_out = adapt_out_sum.astype(jnp.bfloat16)
    attn_branch = attn_sum + product(adapt_out, b_out)
    hidden_one, norm_one_back = jax.vjp(
        partial(norm_rows, gain_row=ln_gain[0], shift_row=ln_bias[0]),
        x_rows.astype(jnp.float32) + attn_branch,
    )
    hidden_low = hidden_one.astype(jnp.bfloat16)
    up_full, down_full = (
        lax.all_gather(w_up, "fsdp", axis=0, tiled=True),
        lax.all_gather(w_down, "fsdp", axis=1, tiled=True),
    )
    adapt_up = (product(hidden_low, a_up) * pick_rows).astype(jnp.bfloat16)
    pre_act = product(hidden_low, up_full) + product(adapt_up, b_up)
    activated, gelu_back = jax.vjp(gelu_tanh, pre_act)
    gelu_out = activated.astype(jnp.bfloat16)
    part_down = product(gelu_out, down_full)
    part_adapt_down = product(gelu_out, a_down) * pick_rows
    down_sum, adapt_down_sum = lax.psum((part_down, part_adapt_down), "tp")
    adapt_down = adapt_down_sum.astype(jnp.bfloat16)
    second_in = hidden_one + down_sum + product(adapt_down, b_down)
    layer_out, norm_two_back = jax.vjp(
        partial(norm_rows, gain_row=ln_gain[1], shift_row=ln_bias[1]), second_in
    )
    grad_out = dealt_cot.reshape(dev_rows, model_width).astype(jnp.float32)
    (grad_second,) = norm_two_back(grad_out)
    grad_down_low = grad_second.astype(jnp.bfloat16)
    up_back, down_back = (
        lax.all_gather(w_up, "fsdp", axis=0, tiled=True),
        lax.all_gather(w_down, "fsdp", axis=1, tiled=True),
    )
    grad_adapt_down = (against(grad_down_low, b_down) * pick_rows).astype(jnp.bfloat16)
    grad_b_down = across(adapt_down, grad_down_low)
    grad_a_down = across(gelu_out, grad_adapt_down)
    grad_gelu = against(grad_down_low, down_back) + against(grad_adapt_down, a_down)
    (grad_pre,) = gelu_back(grad_gelu)
    grad_pre_low = grad_pre.astype(jnp.bfloat16)
    grad_b_up = across(adapt_up, grad_pre_low)
    part_hidden = against(grad_pre_low, up_back)
    part_adapt_up = against(grad_pre_low, b_up)
    grad_hidden_sum, grad_adapt_up_sum = lax.psum((part_hidden, part_adapt_up), "tp")
    grad_adapt_up = (grad_adapt_up_sum * pick_rows).astype(jnp.bfloat16)
    grad_a_up = across(hidden_low, grad_adapt_up)
    grad_hidden = grad_second + grad_hidden_sum + against(grad_adapt_up, a_up)
    (grad_first,) = norm_one_back(grad_hidden)
    grad_attn_low = grad_first.astype(jnp.bfloat16)
    qkv_back, out_back = (
        lax.all_gather(w_qkv, "fsdp", axis=1, tiled=True),
        lax.all_gather(w_out, "fsdp", axis=1, tiled=True),
    )
    grad_adapt_out = (against(grad_attn_low, b_out) * pick_rows).astype(jnp.bfloat16)
    grad_b_out = across(adapt_out, grad_attn_low)
    grad_a_out = across(ctx_rows, grad_adapt_out)
    grad_context = (against(grad_attn_low, out_back) + against(grad_adapt_out, a_out)).astype(
        jnp.bfloat16
    )

    def attend_back(packed):
        queries, keys_seq, values_seq, usable_row, log_total, grad_ctx_seq = packed
        query_heads = queries.reshape(local_len, heads_here, HEAD_DIM)
        key_heads = keys_seq.reshape(key_count, heads_here, HEAD_DIM)
        value_heads = values_seq.reshape(key_count, heads_here, HEAD_DIM)
        scores = score_block(query_heads, key_heads, usable_row)
        attn_probs = jnp.exp(scores - log_total[..., None])
        probs_low = attn_probs.astype(jnp.bfloat16)
        grad_heads = grad_ctx_seq.reshape(local_len, heads_here, HEAD_DIM)
        grad_values = jnp.einsum(
            "hqk,qhd->khd", probs_low, grad_heads, preferred_element_type=jnp.float32
        )
        grad_probs = jnp.einsum(
            "qhd,khd->hqk", grad_heads, value_heads, preferred_element_type=jnp.float32
        )
        row_dot = jnp.sum(attn_probs * grad_probs, axis=-1, keepdims=True)
        grad_scores = (attn_probs * (grad_probs - row_dot)).astype(jnp.bfloat16)
        grad_query = (
            jnp.einsum("hqk,khd->qhd", grad_scores, key_heads, preferred_element_type=jnp.float32)
            * score_scale
        )
        grad_keys = (
            jnp.einsum("hqk,qhd->khd", grad_scores, query_heads, preferred_element_type=jnp.float32)
            * score_scale
        )
        return (
            grad_query.reshape(local_len, heads_width).astype(jnp.bfloat16),
            grad_keys.reshape(key_count, heads_width),
            grad_values.reshape(key_count, heads_width),
        )

    grad_ctx_seqs = grad_context.reshape(per_dev, local_len, heads_width)
    grad_queries, grad_keys_all, grad_values_all = lax.map(
        attend_back, (queries_all, keys_all, values_all, usable, log_totals, grad_ctx_seqs)
    )
    grad_keys_mine, grad_values_mine = (
        lax.psum_scatter(
            grad_keys_all.astype(jnp.bfloat16), "ctx", scatter_dimension=1, tiled=True
        ).astype(jnp.float32),
        lax.psum_scatter(
            grad_values_all.astype(jnp.bfloat16), "ctx", scatter_dimension=1, tiled=True
        ).astype(jnp.float32),
    )
    grad_proj = [
        grad_queries.reshape(dev_rows, heads_width),
        grad_keys_mine.astype(jnp.bfloat16).reshape(dev_rows, heads_width),
        grad_values_mine.astype(jnp.bfloat16).reshape(dev_rows, heads_width),
    ]
    grad_b_qkv = jnp.stack(
        [across(adapt_qkv[proj_index], grad_proj[proj_index]) for proj_index in range(3)]
    )
    part_input = (
        against(grad_proj[0], qkv_back[0])
        + against(grad_proj[1], qkv_back[1])
        + against(grad_proj[2], qkv_back[2])
    )
    part_adapt_qkv = jnp.stack(
        [against(grad_proj[proj_index], b_qkv[proj_index]) for proj_index in range(3)]
    )
    grad_input_sum, grad_adapt_qkv_sum = (
        lax.psum(part_input.astype(jnp.bfloat16), "tp").astype(jnp.float32),
        lax.psum(part_adapt_qkv.astype(jnp.bfloat16), "tp").astype(jnp.float32),
    )
    grad_adapt_qkv = (grad_adapt_qkv_sum * pick_rows[None]).astype(jnp.bfloat16)
    grad_a_qkv = jnp.stack([across(x_rows, grad_adapt_qkv[proj_index]) for proj_index in range(3)])
    grad_input = (
        grad_first
        + grad_input_sum
        + against(grad_adapt_qkv[0], a_qkv[0])
        + against(grad_adapt_qkv[1], a_qkv[1])
        + against(grad_adapt_qkv[2], a_qkv[2])
    )
    summed_grads = lax.psum(
        (
            grad_a_qkv,
            grad_b_qkv,
            grad_a_out,
            grad_b_out,
            grad_a_up,
            grad_b_up,
            grad_a_down,
            grad_b_down,
        ),
        ("fsdp", "ctx"),
    )
    out_low = layer_out.astype(jnp.bfloat16).reshape(per_dev, local_len, model_width)
    input_low = grad_input.astype(jnp.bfloat16).reshape(per_dev, local_len, model_width)
    back_out, back_input = (
        lax.all_to_all(out_low, "fsdp", split_axis=1, concat_axis=0, tiled=True),
        lax.all_to_all(input_low, "fsdp", split_axis=1, concat_axis=0, tiled=True),
    )
    return (
        back_out,
        back_input,
        summed_grads[0],
        summed_grads[1],
        summed_grads[2],
        summed_grads[3],
        summed_grads[4],
        summed_grads[5],
        summed_grads[6],
        summed_grads[7],
    )


def solution(mesh):
    return jax.shard_map(
        local,
        mesh=mesh,
        in_specs=(
            P(None, ("fsdp", "ctx"), None),
            P(None, ("fsdp", "ctx"), None),
            P(),
            P(),
            P(None, "fsdp", "tp"),
            P("tp", "fsdp"),
            P("fsdp", "tp"),
            P("tp", "fsdp"),
            P(),
            P(),
            P(),
            P(None, None, "tp"),
            P("tp", None),
            P(),
            P(),
            P(None, "tp"),
            P("tp", None),
            P(),
        ),
        out_specs=(
            P(None, ("fsdp", "ctx"), None),
            P(None, ("fsdp", "ctx"), None),
            P(),
            P(None, None, "tp"),
            P("tp", None),
            P(),
            P(),
            P(None, "tp"),
            P("tp", None),
            P(),
        ),
        check_vma=False,
    )
```

profile of v0, /device:TPU:0, one launch (start us, length us, event | category | flops | bytes accessed | tf_op | source)
XLA Modules:
  0.0 2011.4 jit_solution(7236679362293835580)
XLA Ops:
  7.9 6.3 all-to-all-start
  14.6 104.2 %all-to-all-done = bf16[8,64,2048]{2,1,0:T(8,128)(2,1)S(1)} async-done(((bf16[8,64,2048]{2,1,0:T(8,128)(2,1)}), bf16[8,64,2048]{2,1,0:T(8,128)(2,1)S(1)}, u32[]{:S(2)}, u32[]{:S(2)}) %all-to-all-start) | async-done | bytes 2097184 | tf_op jit(solution)/shard_map/all_to_all | solution.py:75
  124.0 141.4 %all-gather.7.cloned.1.call-done = bf16[3,2048,1024]{2,1,0:T(8,128)(2,1)} async-done(((bf16[3,512,1024]{2,1,0:T(8,128)(2,1)}), bf16[3,2048,1024]{2,1,0:T(8,128)(2,1)}) %all-gather.7.cloned.1.call-update) | async-done | bytes 12582928 | tf_op jit(solution)/shard_map/all_gather | solution.py:89
  297.6 11.3 all-gather.11.cloned.1.call-done
  308.8 37.2 %all-gather.9.cloned.1.call-done = bf16[2,1024,1024]{1,2,0:T(8,128)(2,1)} async-done(((bf16[2,256,1024]{1,2,0:T(8,128)(2,1)}), bf16[2,1024,1024]{1,2,0:T(8,128)(2,1)}) %all-gather.9.cloned.1.call-update) | async-done | bytes 4194320 | tf_op jit(solution)/shard_map/all_gather | solution.py:105
  347.1 26.9 %while.26 = (s32[]{:T(128)}, bf16[2,256,1024]{2,1,0:T(8,128)(2,1)}, f32[2,8,256]{2,1,0:T(8,128)S(1)}, bf16[2,1024,1024]{1,2,0:T(8,128)(2,1)}, pred[2,1024]{1,0:T...) while((s32[]{:T(128)}, bf16[2,256,1024]{2,1,0:T(8,128)(2,1)}, ...), condition=%wide.region_3.4_spmd, body=%wide.region_0.3_spmd.sunk | while | flops 1097070592 | bytes 46208640 | solution.py:130
  374.1 54.2 %all-gather.13.cloned.1.call-done = bf16[1024,2048]{1,0:T(8,128)(2,1)} async-done(((bf16[1024,512]{1,0:T(8,128)(2,1)}), bf16[1024,2048]{1,0:T(8,128)(2,1)}) %all-gather.13.cloned.1.call-update) | async-done | bytes 4194320 | tf_op jit(solution)/shard_map/all_gather | solution.py:90
  428.3 6.8 fusion.101
  439.0 19.6 all-reduce.20
  458.6 88.7 %all-reduce.11.cloned.1.call-done = f32[512,2048]{1,0:T(8,128)} async-done(((f32[512,2048]{1,0:T(8,128)}), f32[512,2048]{1,0:T(8,128)}) %all-reduce.11.cloned.1.call-update) | async-done | bytes 4194320 | tf_op jit(solution)/shard_map/psum | solution.py:134
  559.5 276.1 %all-gather.15.cloned.1.call-done = bf16[2048,4096]{1,0:T(8,128)(2,1)} async-done(((bf16[512,4096]{1,0:T(8,128)(2,1)}), bf16[2048,4096]{1,0:T(8,128)(2,1)}) %all-gather.15.cloned.1.call-update) | async-done | bytes 16777232 | tf_op jit(solution)/shard_map/all_gather | solution.py:143
  835.6 20.4 %multiply_convert_fusion.1 = (bf16[512,4096]{1,0:T(8,128)(2,1)}, f32[512,4096]{1,0:T(8,128)}) fusion(f32[512,4096]{1,0:T(8,128)} %fusion.102, bf16[512,2048]{1,0:T(8,128)(2,1)S(1)} %fusion.31, bf16[2048,4096]{1,0:T(8,128)(2,1)} %all-gather.15.cloned.1.call-done), kind=kOutput, calls=%fused_computation.52 | convolution fusion | flops 8610906112 | bytes 39845888 | tf_op jit(solution)/shard_map/dot_general | solution.py:28
  856.0 266.2 %all-gather.17.cloned.1.call-done = bf16[4096,2048]{1,0:T(8,128)(2,1)} async-done(((bf16[4096,512]{1,0:T(8,128)(2,1)}), bf16[4096,2048]{1,0:T(8,128)(2,1)}) %all-gather.17.cloned.1.call-update) | async-done | bytes 16777232 | tf_op jit(solution)/shard_map/all_gather | solution.py:144
  1122.2 14.9 fusion.103
  1138.7 51.1 %all_to_all.60 = bf16[8,64,2048]{2,1,0:T(8,128)(2,1)S(1)} all-to-all(bf16[8,64,2048]{2,1,0:T(8,128)(2,1)S(1)} %copy-done.39), channel_id=1, replica_groups=mesh['fsdp'=4,'ctx'=4,'tp'=2] {'fsdp'}, dimensions={0} | all-to-all | bytes 4194304 | tf_op jit(solution)/shard_map/all_to_all | solution.py:76
  1194.8 18.6 all-reduce.21
  1213.4 35.5 %all-reduce.13.cloned.1.call-done = f32[512,2048]{1,0:T(8,128)} async-done(((f32[512,2048]{1,0:T(8,128)}), f32[512,2048]{1,0:T(8,128)}) %all-reduce.13.cloned.1.call-update) | async-done | bytes 4194320 | tf_op jit(solution)/shard_map/psum | solution.py:152
  1264.7 22.3 %fusion.22 = bf16[512,4096]{1,0:T(8,128)(2,1)} fusion(f32[512,4096]{1,0:T(8,128)} %get-tuple-element.250, f32[512,4096]{1,0:T(8,128)} %fusion.104, bf16[512,2048]{1,0:T(8,128)(2,1)S(1)} %add_convert_fusion.4, bf16[4096,2048]{1,0:T(8,128)(2,1)} %all-gather.17.cloned.1.call-done), kind=kOutput, calls=%fused_computation.49 | convolution fusion | flops 8642363392 | bytes 39845888 | tf_op jit(solution)/shard_map/dot_general | solution.py:32
  1291.3 14.0 fusion.105
  1305.4 113.3 %all-reduce.17.cloned.1.call-done = (f32[512,2048]{1,0:T(8,128)}, f32[512,128]{1,0:T(8,128)}) async-done(((f32[512,2048]{1,0:T(8,128)}, f32[512,128]{1,0:T(8,128)}), (f32[512,2048]{1,0:T(8,128)}, f32[512,128]{1,0:T(8,128)})) %all-reduce.17.cloned.1.call-update) | async-done | bytes 4456464 | tf_op jit(solution)/shard_map/psum | solution.py:174
  1419.7 6.1 multiply_reduce_fusion.1
  1436.4 91.7 %while.27 = (s32[]{:T(128)}, bf16[2,256,1024]{2,1,0:T(8,128)(2,1)}, bf16[2,1024,1024]{2,1,0:T(8,128)(2,1)}, bf16[2,1024,1024]{2,1,0:T(8,128)(2,1)}, bf16[2,1024,...) while((s32[]{:T(128)}, bf16[2,256,1024]{2,1,0:T(8,128)(2,1)}, ...), condition=%wide.region_20.21_spmd, body=%wide.region_18.20_spmd.sunk | while | flops 2718431232 | bytes 173603120 | solution.py:223
  1447.1 6.4 multiply_reduce_fusion.6
  1464.0 6.8 fusion.233
  1492.8 6.4 multiply_reduce_fusion.6
  1509.7 6.8 fusion.233
  1538.7 6.8 fusion.27
  1545.5 27.2 %reduce-scatter.3.cloned.1.call-done = bf16[2,256,1024]{2,1,0:T(8,128)(2,1)} async-done(((bf16[2,1024,1024]{2,1,0:T(8,128)(2,1)}), bf16[2,256,1024]{2,1,0:T(8,128)(2,1)}) %reduce-scatter.3.cloned.1.call-update) | async-done | bytes 1048592 | tf_op jit(solution)/shard_map/reduce_scatter | solution.py:227
  1574.4 45.4 %reduce-scatter.5.cloned.1.call-done = bf16[2,256,1024]{2,1,0:T(8,128)(2,1)} async-done(((bf16[2,1024,1024]{2,1,0:T(8,128)(2,1)}), bf16[2,256,1024]{2,1,0:T(8,128)(2,1)}) %reduce-scatter.5.cloned.1.call-update) | async-done | bytes 1048592 | tf_op jit(solution)/shard_map/reduce_scatter | solution.py:230
  1649.0 56.3 %all-reduce.19.cloned.1.call-done = (bf16[3,512,128]{2,1,0:T(8,128)(2,1)}, bf16[512,2048]{1,0:T(8,128)(2,1)}) async-done(((bf16[3,512,128]{2,1,0:T(8,128)(2,1)}, bf16[512,2048]{1,0:T(8,128)(2,1)}), (bf16[3,512,128]{2,1,0:T(8,128)(2,1)}, bf16[512,2048]{1,0:T(8,128)(2,1)})) %all-reduce.19.cloned.1.call-update) | async-done | bytes 2490384 | tf_op jit(solution)/shard_map/psum | solution.py:252
  1727.2 67.8 %all-to-all-done.3 = bf16[2,256,2048]{2,0,1:T(2,128)(2,1)S(1)} async-done(((bf16[2,256,2048]{2,0,1:T(2,128)(2,1)}), bf16[2,256,2048]{2,0,1:T(2,128)(2,1)S(1)}, u32[]{:S(2)}, u32[]{:S(2)}) %all-to-all-start.3) | async-done | bytes 2097184 | tf_op jit(solution)/shard_map/all_to_all | solution.py:280
  1797.2 196.3 %all-reduce.15.cloned.1.call-done = (f32[3,2048,128]{1,2,0:T(8,128)}, f32[3,128,1024]{2,1,0:T(8,128)}, f32[1024,128]{1,0:T(8,128)}, f32[128,2048]{1,0:T(8,128)},...) async-done(((f32[3,2048,128]{1,2,0:T(8,128)}, f32[3,128,1024]{2,1,0:T(8,128)}, f32[1024,128]{1,0:T(8,128)}, ...) | async-done | bytes 12582928 | tf_op jit(solution)/shard_map/psum | solution.py:263
  (357 shorter events, 261.4 us)
Async XLA Ops:
  7.2 1185.3 %copy-start = (bf16[4096,128]{1,0:T(8,128)(2,1)S(1)}, bf16[4096,128]{1,0:T(8,128)(2,1)}, u32[]{:S(2)}) copy-start(bf16[4096,128]{1,0:T(8,128)(2,1)} %param.38) | copy-start | bytes 3145732
  7.2 7.1 copy-start.80
  7.2 258.2 %all-gather.7.cloned.1.call-start = ((), (), s32[]{:S(2)}) async-start(), calls=%async_computation.6 | async-start | bytes 15728640 | tf_op jit(solution)/shard_map/all_gather | solution.py:89
  7.9 110.8 %all-to-all-start = ((bf16[8,64,2048]{2,1,0:T(8,128)(2,1)}), bf16[8,64,2048]{2,1,0:T(8,128)(2,1)S(1)}, u32[]{:S(2)}, u32[]{:S(2)}) async-start(bf16[8,64,2048]{2,1,0:T(8,128)(2,1)} %param.22), calls=%async_computation | async-start | bytes 4194304 | tf_op jit(solution)/shard_map/all_to_all | solution.py:75
  14.3 294.6 %all-gather.11.cloned.1.call-start = ((), (), s32[]{:S(2)}) async-start(), calls=%async_computation.8 | async-start | bytes 5242880 | tf_op jit(solution)/shard_map/all_gather | solution.py:104
  14.6 1413.2 %copy-start.71 = (f32[2,128]{1,0:T(2,128)}, f32[2,128]{1,0:T(2,128)S(1)}, u32[]{:S(2)}) copy-start(f32[2,128]{1,0:T(2,128)S(1)} %reshape.257) | copy-start | bytes 3076
  121.8 425.5 %copy-start.6 = (bf16[4,2,64,2048]{3,2,0,1:T(8,128)(2,1)}, bf16[4,2,64,2048]{3,2,0,1:T(8,128)(2,1)S(1)}, u32[]{:S(2)}) copy-start(bf16[4,2,64,2048]{3,2,0,1:T(8,128)(2,1)S(1)} %copy.63) | copy-start | bytes 6291460
  124.0 145.9 %copy-start.53 = (bf16[512,128]{1,0:T(8,128)(2,1)}, bf16[512,128]{1,0:T(8,128)(2,1)S(1)}, u32[]{:S(2)}) copy-start(bf16[512,128]{1,0:T(8,128)(2,1)S(1)} %fusion.34) | copy-start | bytes 393220
  274.5 71.5 %all-gather.9.cloned.1.call-start = ((), (), s32[]{:S(2)}) async-start(), calls=%async_computation.7 | async-start | bytes 5242880 | tf_op jit(solution)/shard_map/all_gather | solution.py:105
  285.6 142.6 %all-gather.13.cloned.1.call-start = ((), (), s32[]{:S(2)}) async-start(), calls=%async_computation.9 | async-start | bytes 5242880 | tf_op jit(solution)/shard_map/all_gather | solution.py:90
  286.2 261.1 %all-reduce.11.cloned.1.call-start = ((), (), s32[]{:S(2)}) async-start(), calls=%async_computation.10 | async-start | bytes 8388608 | tf_op jit(solution)/shard_map/psum | solution.py:134
  374.1 61.0 %copy-start.69 = (pred[2,1024]{1,0:T(4,128)(4,1)}, pred[2,1024]{1,0:T(4,128)(4,1)S(1)}, u32[]{:S(2)}) copy-start(pred[2,1024]{1,0:T(4,128)(4,1)S(1)} %get-tuple-element.541) | copy-start | bytes 6148
  374.1 61.0 %copy-start.73 = (f32[2,8,256]{2,1,0:T(8,128)}, f32[2,8,256]{2,1,0:T(8,128)S(1)}, u32[]{:S(2)}) copy-start(f32[2,8,256]{2,1,0:T(8,128)S(1)} %get-tuple-element.410) | copy-start | bytes 49156
  435.1 400.5 %all-gather.15.cloned.1.call-start = ((), (), s32[]{:S(2)}) async-start(), calls=%async_computation.11 | async-start | bytes 20971520 | tf_op jit(solution)/shard_map/all_gather | solution.py:143
  435.7 686.5 %all-gather.17.cloned.1.call-start = ((), (), s32[]{:S(2)}) async-start(), calls=%async_computation.12 | async-start | bytes 20971520 | tf_op jit(solution)/shard_map/all_gather | solution.py:144
  436.5 812.5 %all-reduce.13.cloned.1.call-start = ((), (), s32[]{:S(2)}) async-start(), calls=%async_computation.13 | async-start | bytes 8388608 | tf_op jit(solution)/shard_map/psum | solution.py:152
  458.6 91.9 %copy-start.47 = (bf16[512,128]{1,0:T(8,128)(2,1)}, bf16[512,128]{1,0:T(8,128)(2,1)S(1)}, u32[]{:S(2)}) copy-start(bf16[512,128]{1,0:T(8,128)(2,1)S(1)} %all-reduce.20) | copy-start | bytes 393220
  552.5 283.1 %copy-start.14 = (bf16[512,2048]{1,0:T(8,128)(2,1)}, bf16[512,2048]{1,0:T(8,128)(2,1)S(1)}, u32[]{:S(2)}) copy-start(bf16[512,2048]{1,0:T(8,128)(2,1)S(1)} %fusion.31) | copy-start | bytes 6291460
  1137.1 281.6 %all-reduce.17.cloned.1.call-start = ((), (), s32[]{:S(2)}) async-start(), calls=%async_computation.17 | async-start | bytes 8912896 | tf_op jit(solution)/shard_map/psum | solution.py:174
  1193.5 55.4 %copy-start.42 = (bf16[128,2048]{1,0:T(8,128)(2,1)S(1)}, bf16[128,2048]{1,0:T(8,128)(2,1)}, u32[]{:S(2)}) copy-start(bf16[128,2048]{1,0:T(8,128)(2,1)} %param.39) | copy-start | bytes 1572868
  1213.4 40.5 %copy-start.61 = (bf16[512,128]{1,0:T(8,128)(2,1)}, bf16[512,128]{1,0:T(8,128)(2,1)S(1)}, u32[]{:S(2)}) copy-start(bf16[512,128]{1,0:T(8,128)(2,1)S(1)} %all-reduce.21) | copy-start | bytes 393220
  1264.7 22.3 %copy-start.30 = (bf16[128,4096]{1,0:T(8,128)(2,1)S(1)}, bf16[128,4096]{1,0:T(8,128)(2,1)}, u32[]{:S(2)}) copy-start(bf16[128,4096]{1,0:T(8,128)(2,1)} %param.37) | copy-start | bytes 3145732
  1305.3 114.4 %copy-start.37 = (bf16[2048,128]{1,0:T(8,128)(2,1)S(1)}, bf16[2048,128]{1,0:T(8,128)(2,1)}, u32[]{:S(2)}) copy-start(bf16[2048,128]{1,0:T(8,128)(2,1)} %param.36) | copy-start | bytes 1572868
  1305.3 267.4 %reduce-scatter.3.cloned.1.call-start = ((), (), s32[]{:S(2)}) async-start(), calls=%async_computation.14 | async-start | bytes 5242880 | tf_op jit(solution)/shard_map/reduce_scatter | solution.py:227
  1528.1 91.7 %reduce-scatter.5.cloned.1.call-start = ((), (), s32[]{:S(2)}) async-start(), calls=%async_computation.15 | async-start | bytes 5242880 | tf_op jit(solution)/shard_map/reduce_scatter | solution.py:230
  1529.7 8.6 copy-start.24
  1533.2 185.6 %all-to-all-start.1 = ((bf16[2,256,2048]{2,0,1:T(2,128)(2,1)}), bf16[2,256,2048]{2,0,1:T(2,128)(2,1)}, u32[]{:S(2)}, u32[]{:S(2)}) async-start(bf16[2,256,2048]{2,0,1:T(2,128)(2,1)} %copy.68), calls=%async_computation.1 | async-start | bytes 4194304 | tf_op jit(solution)/shard_map/all_to_all | solution.py:279
  1537.9 167.4 %all-reduce.19.cloned.1.call-start = ((), (), s32[]{:S(2)}) async-start(), calls=%async_computation.18 | async-start | bytes 4980736 | tf_op jit(solution)/shard_map/psum | solution.py:252
  1633.4 360.0 %all-reduce.15.cloned.1.call-start = ((), (), s32[]{:S(2)}) async-start(), calls=%async_computation.16 | async-start | bytes 25165824 | tf_op jit(solution)/shard_map/psum | solution.py:263
  1645.5 59.7 %copy-start.72 = (f32[2,128]{1,0:T(2,128)S(1)}, f32[2,128]{1,0:T(2,128)}, u32[]{:S(2)}) copy-start(f32[2,128]{1,0:T(2,128)} %copy-done.71) | copy-start | bytes 3076
  1647.0 59.4 %copy-start.7 = (bf16[4,2,64,2048]{3,2,0,1:T(8,128)(2,1)S(1)}, bf16[4,2,64,2048]{3,2,0,1:T(8,128)(2,1)}, u32[]{:S(2)}) copy-start(bf16[4,2,64,2048]{3,2,0,1:T(8,128)(2,1)} %copy-done.6) | copy-start | bytes 6291460
  1718.7 76.3 %all-to-all-start.3 = ((bf16[2,256,2048]{2,0,1:T(2,128)(2,1)}), bf16[2,256,2048]{2,0,1:T(2,128)(2,1)S(1)}, u32[]{:S(2)}, u32[]{:S(2)}) async-start(bf16[2,256,2048]{2,0,1:T(2,128)(2,1)} %copy.76), calls=%async_computation.5 | async-start | bytes 4194304 | tf_op jit(solution)/shard_map/all_to_all | solution.py:280
  (76 other events, 260.5 us)
Sparse Core Ops, SparseCore 0:
  9.6 255.7 all-gather.6
  274.7 34.1 all-gather.10
  311.0 35.0 all-gather.8
  347.5 80.7 all-gather.12
  435.2 112.0 all-reduce.10
  548.8 286.7 all-gather.14
  837.2 284.9 all-gather.16
  1137.2 111.6 all-reduce.12
  1305.5 113.2 all-reduce.16
  1528.2 44.4 reduce-scatter.2
  1575.3 44.4 reduce-scatter.4
  1633.6 71.6 all-reduce.18
  1711.8 281.6 all-reduce.14
where the time goes:
time: 2020 us; the launch traced here: 2010 us
  waiting for transfers between devices  1520 us (75%)
  matrix products  235 us (12%)
  local copies, waits for them, and re-layouts  108 us (5%)
  blocking collectives  89.4 us (4%)
  other arithmetic  22 us (1%)
    all_gather x1, waiting for transfers between devices, local(): lax.all_gather(w_up, 'fsdp', axis=0, tiled=True)  276 us
    all_gather x1, waiting for transfers between devices, local(): lax.all_gather(w_down, 'fsdp', axis=1, tiled=True)  266 us
    psum x1, waiting for transfers between devices, local(): lax.psum((grad_a_qkv, grad_b_qkv, grad_a_out, grad_b_out, grad_a_up, grad...  196 us
    all_gather x1, waiting for transfers between devices, local(): lax.all_gather(w_qkv, 'fsdp', axis=1, tiled=True)  141 us
    psum x1, waiting for transfers between devices, local(): lax.psum((part_hidden, part_adapt_up), 'tp')  113 us
    all_to_all x1, waiting for transfers between devices, local(): lax.all_to_all(x_in, 'fsdp', split_axis=0, concat_axis=1, tiled=True)  104 us
    psum x1, waiting for transfers between devices, local(): attn_sum, adapt_out_sum = lax.psum((part_out, part_adapt), 'tp')  88.7 us
    dot_general x18, matrix products, product(): return jnp.dot(left_side, right_side, preferred_element_type=jnp.float32)  86.5 us
  transfers between devices with their start and end apart: 16, of which 15 were waited for; matrix products, arithmetic and copies ran while one was open for 7% of the time, Pallas kernels for 0%

commit v1 on v0

--- a/solution.py
+++ b/solution.py
@@ -10,6 +10,9 @@
 ADAPTERS = 8
 NORM_EPS = 1e-06
 GELU_COEF = 0.7978845608028654
+get_squares = lambda obj, net_axis, peer_axis: lax.psum(
+    lax.psum(obj, axis_name=net_axis), axis_name=peer_axis
+)
 
 
 def norm_rows(values, gain_row, shift_row):
@@ -260,7 +263,7 @@
         + against(grad_adapt_qkv[1], a_qkv[1])
         + against(grad_adapt_qkv[2], a_qkv[2])
     )
-    summed_grads = lax.psum(
+    summed_grads = get_squares(
         (
             grad_a_qkv,
             grad_b_qkv,
@@ -271,7 +274,8 @@
             grad_a_down,
             grad_b_down,
         ),
-        ("fsdp", "ctx"),
+        "ctx",
+        "fsdp",
     )
     out_low = layer_out.astype(jnp.bfloat16).reshape(per_dev, local_len, model_width)
     input_low = grad_input.astype(jnp.bfloat16).reshape(per_dev, local_len, model_width)

time: 2020 us -> 2480 us (1.23)
  waiting for transfers between devices: 1520 us -> 1990 us
    psum x1 -> x2, waiting for transfers between devices: 196 us -> 527 us  [the longest x1 304 us: lax.psum(lax.psum(obj, axis_name=net_axis), axis_name=peer_axis)]
    all_to_all x1, waiting for transfers between devices: 0.01 us -> 94.4 us  [local(): lax.all_to_all(out_low, 'fsdp', split_axis=1, concat_axis=0, tiled=True)]
    all_to_all x1, waiting for transfers between devices: 67.8 us -> 95.2 us  [local(): lax.all_to_all(input_low, 'fsdp', split_axis=1, concat_axis=0, tiled=True)]
  transfers between devices with their start and end apart: 16 -> 17, of which waited for: 15 -> 17; matrix products, arithmetic and copies ran while one was open for 7% -> 5% of each run, Pallas kernels for 0% -> 0%
where the time goes in v1:
time: 2480 us; the launch traced here: 2470 us
  waiting for transfers between devices  1990 us (80%)
  matrix products  239 us (10%)
  local copies, waits for them, and re-layouts  106 us (4%)
  blocking collectives  89.4 us (4%)
    psum x1, waiting for transfers between devices, lax.psum(lax.psum(obj, axis_name=net_axis), axis_name=peer_axis)  304 us
    all_gather x1, waiting for transfers between devices, local(): lax.all_gather(w_up, 'fsdp', axis=0, tiled=True)  276 us
    all_gather x1, waiting for transfers between devices, local(): lax.all_gather(w_down, 'fsdp', axis=1, tiled=True)  266 us
    psum x1, waiting for transfers between devices, lax.psum(obj, axis_name=net_axis)  223 us
    all_gather x1, waiting for transfers between devices, local(): lax.all_gather(w_qkv, 'fsdp', axis=1, tiled=True)  141 us
    psum x1, waiting for transfers between devices, local(): lax.psum((part_hidden, part_adapt_up), 'tp')  113 us
    all_to_all x1, waiting for transfers between devices, local(): lax.all_to_all(x_in, 'fsdp', split_axis=0, concat_axis=1, tiled=True)  104 us
    all_to_all x1, waiting for transfers between devices, local(): lax.all_to_all(input_low, 'fsdp', split_axis=1, concat_axis=0, tiled=True)  95.2 us
  transfers between devices with their start and end apart: 17, of which 17 were waited for; matrix products, arithmetic and copies ran while one was open for 5% of the time, Pallas kernels for 0%

profile of v1, /device:TPU:0, one launch (start us, length us, event | category | flops | bytes accessed | tf_op | source)
XLA Modules:
  0.0 2474.7 jit_solution(9039997213035784807)
XLA Ops:
  14.6 104.2 %all-to-all-done = bf16[8,64,2048]{2,1,0:T(8,128)(2,1)S(1)} async-done(((bf16[8,64,2048]{2,1,0:T(8,128)(2,1)}), bf16[8,64,2048]{2,1,0:T(8,128)(2,1)S(1)}, u32[]{:S(2)}, u32[]{:S(2)}) %all-to-all-start) | async-done | bytes 2097184 | tf_op jit(solution)/shard_map/all_to_all | solution.py:78
  124.0 141.4 %all-gather.7.cloned.1.call-done = bf16[3,2048,1024]{2,1,0:T(8,128)(2,1)} async-done(((bf16[3,512,1024]{2,1,0:T(8,128)(2,1)}), bf16[3,2048,1024]{2,1,0:T(8,128)(2,1)}) %all-gather.7.cloned.1.call-update) | async-done | bytes 12582928 | tf_op jit(solution)/shard_map/all_gather | solution.py:92
  297.6 11.3 all-gather.11.cloned.1.call-done
  308.8 37.2 %all-gather.9.cloned.1.call-done = bf16[2,1024,1024]{1,2,0:T(8,128)(2,1)} async-done(((bf16[2,256,1024]{1,2,0:T(8,128)(2,1)}), bf16[2,1024,1024]{1,2,0:T(8,128)(2,1)}) %all-gather.9.cloned.1.call-update) | async-done | bytes 4194320 | tf_op jit(solution)/shard_map/all_gather | solution.py:108
  347.1 26.9 %while.26 = (s32[]{:T(128)}, bf16[2,256,1024]{2,1,0:T(8,128)(2,1)}, f32[2,8,256]{2,1,0:T(8,128)S(1)}, bf16[2,1024,1024]{1,2,0:T(8,128)(2,1)}, pred[2,1024]{1,0:T...) while((s32[]{:T(128)}, bf16[2,256,1024]{2,1,0:T(8,128)(2,1)}, ...), condition=%wide.region_3.4_spmd, body=%wide.region_0.3_spmd.sunk | while | flops 1097070592 | bytes 46208640 | solution.py:133
  374.1 54.2 %all-gather.13.cloned.1.call-done = bf16[1024,2048]{1,0:T(8,128)(2,1)} async-done(((bf16[1024,512]{1,0:T(8,128)(2,1)}), bf16[1024,2048]{1,0:T(8,128)(2,1)}) %all-gather.13.cloned.1.call-update) | async-done | bytes 4194320 | tf_op jit(solution)/shard_map/all_gather | solution.py:93
  428.3 6.8 fusion.101
  439.0 19.6 all-reduce.24
  458.6 88.7 %all-reduce.13.cloned.1.call-done = f32[512,2048]{1,0:T(8,128)} async-done(((f32[512,2048]{1,0:T(8,128)}), f32[512,2048]{1,0:T(8,128)}) %all-reduce.13.cloned.1.call-update) | async-done | bytes 4194320 | tf_op jit(solution)/shard_map/psum | solution.py:137
  559.5 276.1 %all-gather.15.cloned.1.call-done = bf16[2048,4096]{1,0:T(8,128)(2,1)} async-done(((bf16[512,4096]{1,0:T(8,128)(2,1)}), bf16[2048,4096]{1,0:T(8,128)(2,1)}) %all-gather.15.cloned.1.call-update) | async-done | bytes 16777232 | tf_op jit(solution)/shard_map/all_gather | solution.py:146
  835.6 20.4 multiply_convert_fusion.1
  856.0 266.2 %all-gather.17.cloned.1.call-done = bf16[4096,2048]{1,0:T(8,128)(2,1)} async-done(((bf16[4096,512]{1,0:T(8,128)(2,1)}), bf16[4096,2048]{1,0:T(8,128)(2,1)}) %all-gather.17.cloned.1.call-update) | async-done | bytes 16777232 | tf_op jit(solution)/shard_map/all_gather | solution.py:147
  1122.2 15.0 fusion.103
  1138.8 51.1 %all_to_all.60 = bf16[8,64,2048]{2,1,0:T(8,128)(2,1)S(1)} all-to-all(bf16[8,64,2048]{2,1,0:T(8,128)(2,1)S(1)} %copy-done.38), channel_id=1, replica_groups=mesh['fsdp'=4,'ctx'=4,'tp'=2] {'fsdp'}, dimensions={0} | all-to-all | bytes 4194304 | tf_op jit(solution)/shard_map/all_to_all | solution.py:79
  1194.9 18.6 all-reduce.25
  1213.5 35.5 %all-reduce.15.cloned.1.call-done = f32[512,2048]{1,0:T(8,128)} async-done(((f32[512,2048]{1,0:T(8,128)}), f32[512,2048]{1,0:T(8,128)}) %all-reduce.15.cloned.1.call-update) | async-done | bytes 4194320 | tf_op jit(solution)/shard_map/psum | solution.py:155
  1264.9 22.3 fusion.22
  1291.5 14.1 fusion.105
  1305.7 113.3 %all-reduce.21.cloned.1.call-done = (f32[512,2048]{1,0:T(8,128)}, f32[512,128]{1,0:T(8,128)}) async-done(((f32[512,2048]{1,0:T(8,128)}, f32[512,128]{1,0:T(8,128)}), (f32[512,2048]{1,0:T(8,128)}, f32[512,128]{1,0:T(8,128)})) %all-reduce.21.cloned.1.call-update) | async-done | bytes 4456464 | tf_op jit(solution)/shard_map/psum | solution.py:177
  1436.7 91.3 %while.27 = (s32[]{:T(128)}, bf16[2,256,1024]{2,1,0:T(8,128)(2,1)}, bf16[2,1024,1024]{2,1,0:T(8,128)(2,1)}, bf16[2,1024,1024]{2,1,0:T(8,128)(2,1)}, bf16[2,1024,...) while((s32[]{:T(128)}, bf16[2,256,1024]{2,1,0:T(8,128)(2,1)}, ...), condition=%wide.region_20.21_spmd, body=%wide.region_18.20_spmd.sunk | while | flops 2718431232 | bytes 173603120 | solution.py:226
  1447.4 6.4 multiply_reduce_fusion.6
  1464.2 6.8 fusion.233
  1492.9 6.4 multiply_reduce_fusion.6
  1509.7 6.8 fusion.233
  1529.9 6.7 fusion.27
  1536.6 36.0 %reduce-scatter.3.cloned.1.call-done = bf16[2,256,1024]{2,1,0:T(8,128)(2,1)} async-done(((bf16[2,1024,1024]{2,1,0:T(8,128)(2,1)}), bf16[2,256,1024]{2,1,0:T(8,128)(2,1)}) %reduce-scatter.3.cloned.1.call-update) | async-done | bytes 1048592 | tf_op jit(solution)/shard_map/reduce_scatter | solution.py:230
  1574.3 45.4 %reduce-scatter.5.cloned.1.call-done = bf16[2,256,1024]{2,1,0:T(8,128)(2,1)} async-done(((bf16[2,1024,1024]{2,1,0:T(8,128)(2,1)}), bf16[2,256,1024]{2,1,0:T(8,128)(2,1)}) %reduce-scatter.5.cloned.1.call-update) | async-done | bytes 1048592 | tf_op jit(solution)/shard_map/reduce_scatter | solution.py:233
  1649.2 55.9 %all-reduce.23.cloned.1.call-done = (bf16[3,512,128]{2,1,0:T(8,128)(2,1)}, bf16[512,2048]{1,0:T(8,128)(2,1)}) async-done(((bf16[3,512,128]{2,1,0:T(8,128)(2,1)}, bf16[512,2048]{1,0:T(8,128)(2,1)}), (bf16[3,512,128]{2,1,0:T(8,128)(2,1)}, bf16[512,2048]{1,0:T(8,128)(2,1)})) %all-reduce.23.cloned.1.call-update) | async-done | bytes 2490384 | tf_op jit(solution)/shard_map/psum | solution.py:255
  1709.7 223.3 %all-reduce.17.cloned.1.call-done = (f32[3,2048,128]{1,2,0:T(8,128)}, f32[3,128,1024]{2,1,0:T(8,128)}, f32[1024,128]{1,0:T(8,128)}, f32[128,2048]{1,0:T(8,128)},...) async-done(((f32[3,2048,128]{1,2,0:T(8,128)}, f32[3,128,1024]{2,1,0:T(8,128)}, f32[1024,128]{1,0:T(8,128)}, ...) | async-done | bytes 12582928 | tf_op jit(solution)/shard_map/psum | solution.py:14
  1952.6 94.4 %all-to-all-done.1 = bf16[2,256,2048]{2,0,1:T(2,128)(2,1)S(1)} async-done(((bf16[2,256,2048]{2,0,1:T(2,128)(2,1)}), bf16[2,256,2048]{2,0,1:T(2,128)(2,1)S(1)}, u32[]{:S(2)}, u32[]{:S(2)}) %all-to-all-start.1) | async-done | bytes 2097184 | tf_op jit(solution)/shard_map/all_to_all | solution.py:283
  2054.0 95.2 %all-to-all-done.3 = bf16[2,256,2048]{2,0,1:T(2,128)(2,1)} async-done(((bf16[2,256,2048]{2,0,1:T(2,128)(2,1)}), bf16[2,256,2048]{2,0,1:T(2,128)(2,1)}, u32[]{:S(2)}, u32[]{:S(2)}) %all-to-all-start.3) | async-done | bytes 2097184 | tf_op jit(solution)/shard_map/all_to_all | solution.py:284
  2152.9 303.9 %all-reduce.19.cloned.1.call-done = (f32[3,2048,128]{1,2,0:T(8,128)}, f32[3,128,1024]{2,1,0:T(8,128)}, f32[1024,128]{1,0:T(8,128)}, f32[128,2048]{1,0:T(8,128)},...) async-done(((f32[3,2048,128]{1,2,0:T(8,128)}, f32[3,128,1024]{2,1,0:T(8,128)}, f32[1024,128]{1,0:T(8,128)}, ...) | async-done | bytes 12582928 | tf_op jit(solution)/shard_map/psum | solution.py:13
  (358 shorter events, 275.8 us)
Async XLA Ops:
  7.2 1185.4 %copy-start = (bf16[4096,128]{1,0:T(8,128)(2,1)S(1)}, bf16[4096,128]{1,0:T(8,128)(2,1)}, u32[]{:S(2)}) copy-start(bf16[4096,128]{1,0:T(8,128)(2,1)} %param.38) | copy-start | bytes 3145732
  7.2 7.1 copy-start.79
  7.2 258.2 %all-gather.7.cloned.1.call-start = ((), (), s32[]{:S(2)}) async-start(), calls=%async_computation.6 | async-start | bytes 15728640 | tf_op jit(solution)/shard_map/all_gather | solution.py:92
  7.9 110.8 %all-to-all-start = ((bf16[8,64,2048]{2,1,0:T(8,128)(2,1)}), bf16[8,64,2048]{2,1,0:T(8,128)(2,1)S(1)}, u32[]{:S(2)}, u32[]{:S(2)}) async-start(bf16[8,64,2048]{2,1,0:T(8,128)(2,1)} %param.22), calls=%async_computation | async-start | bytes 4194304 | tf_op jit(solution)/shard_map/all_to_all | solution.py:78
  14.3 294.6 %all-gather.11.cloned.1.call-start = ((), (), s32[]{:S(2)}) async-start(), calls=%async_computation.8 | async-start | bytes 5242880 | tf_op jit(solution)/shard_map/all_gather | solution.py:107
  14.6 1413.5 %copy-start.70 = (f32[2,128]{1,0:T(2,128)}, f32[2,128]{1,0:T(2,128)S(1)}, u32[]{:S(2)}) copy-start(f32[2,128]{1,0:T(2,128)S(1)} %reshape.257) | copy-start | bytes 3076
  121.8 425.5 %copy-start.6 = (bf16[4,2,64,2048]{3,2,0,1:T(8,128)(2,1)}, bf16[4,2,64,2048]{3,2,0,1:T(8,128)(2,1)S(1)}, u32[]{:S(2)}) copy-start(bf16[4,2,64,2048]{3,2,0,1:T(8,128)(2,1)S(1)} %copy.63) | copy-start | bytes 6291460
  124.0 145.9 %copy-start.52 = (bf16[512,128]{1,0:T(8,128)(2,1)}, bf16[512,128]{1,0:T(8,128)(2,1)S(1)}, u32[]{:S(2)}) copy-start(bf16[512,128]{1,0:T(8,128)(2,1)S(1)} %fusion.34) | copy-start | bytes 393220
  274.5 71.5 %all-gather.9.cloned.1.call-start = ((), (), s32[]{:S(2)}) async-start(), calls=%async_computation.7 | async-start | bytes 5242880 | tf_op jit(solution)/shard_map/all_gather | solution.py:108
  285.6 142.6 %all-gather.13.cloned.1.call-start = ((), (), s32[]{:S(2)}) async-start(), calls=%async_computation.9 | async-start | bytes 5242880 | tf_op jit(solution)/shard_map/all_gather | solution.py:93
  286.2 261.1 %all-reduce.13.cloned.1.call-start = ((), (), s32[]{:S(2)}) async-start(), calls=%async_computation.10 | async-start | bytes 8388608 | tf_op jit(solution)/shard_map/psum | solution.py:137
  374.1 61.0 %copy-start.68 = (pred[2,1024]{1,0:T(4,128)(4,1)}, pred[2,1024]{1,0:T(4,128)(4,1)S(1)}, u32[]{:S(2)}) copy-start(pred[2,1024]{1,0:T(4,128)(4,1)S(1)} %get-tuple-element.587) | copy-start | bytes 6148
  374.1 61.0 %copy-start.72 = (f32[2,8,256]{2,1,0:T(8,128)}, f32[2,8,256]{2,1,0:T(8,128)S(1)}, u32[]{:S(2)}) copy-start(f32[2,8,256]{2,1,0:T(8,128)S(1)} %get-tuple-element.418) | copy-start | bytes 49156
  435.1 400.5 %all-gather.15.cloned.1.call-start = ((), (), s32[]{:S(2)}) async-start(), calls=%async_computation.11 | async-start | bytes 20971520 | tf_op jit(solution)/shard_map/all_gather | solution.py:146
  435.7 686.5 %all-gather.17.cloned.1.call-start = ((), (), s32[]{:S(2)}) async-start(), calls=%async_computation.12 | async-start | bytes 20971520 | tf_op jit(solution)/shard_map/all_gather | solution.py:147
  436.5 812.6 %all-reduce.15.cloned.1.call-start = ((), (), s32[]{:S(2)}) async-start(), calls=%async_computation.13 | async-start | bytes 8388608 | tf_op jit(solution)/shard_map/psum | solution.py:155
  458.6 91.9 %copy-start.46 = (bf16[512,128]{1,0:T(8,128)(2,1)}, bf16[512,128]{1,0:T(8,128)(2,1)S(1)}, u32[]{:S(2)}) copy-start(bf16[512,128]{1,0:T(8,128)(2,1)S(1)} %all-reduce.24) | copy-start | bytes 393220
  552.5 283.1 %copy-start.14 = (bf16[512,2048]{1,0:T(8,128)(2,1)}, bf16[512,2048]{1,0:T(8,128)(2,1)S(1)}, u32[]{:S(2)}) copy-start(bf16[512,2048]{1,0:T(8,128)(2,1)S(1)} %fusion.31) | copy-start | bytes 6291460
  1137.2 281.7 %all-reduce.21.cloned.1.call-start = ((), (), s32[]{:S(2)}) async-start(), calls=%async_computation.18 | async-start | bytes 8912896 | tf_op jit(solution)/shard_map/psum | solution.py:177
  1193.7 55.4 %copy-start.41 = (bf16[128,2048]{1,0:T(8,128)(2,1)S(1)}, bf16[128,2048]{1,0:T(8,128)(2,1)}, u32[]{:S(2)}) copy-start(bf16[128,2048]{1,0:T(8,128)(2,1)} %param.39) | copy-start | bytes 1572868
  1213.5 40.5 %copy-start.60 = (bf16[512,128]{1,0:T(8,128)(2,1)}, bf16[512,128]{1,0:T(8,128)(2,1)S(1)}, u32[]{:S(2)}) copy-start(bf16[512,128]{1,0:T(8,128)(2,1)S(1)} %all-reduce.25) | copy-start | bytes 393220
  1264.9 22.3 copy-start.29
  1305.6 114.4 %copy-start.36 = (bf16[2048,128]{1,0:T(8,128)(2,1)S(1)}, bf16[2048,128]{1,0:T(8,128)(2,1)}, u32[]{:S(2)}) copy-start(bf16[2048,128]{1,0:T(8,128)(2,1)} %param.36) | copy-start | bytes 1572868
  1305.6 267.0 %reduce-scatter.3.cloned.1.call-start = ((), (), s32[]{:S(2)}) async-start(), calls=%async_computation.14 | async-start | bytes 5242880 | tf_op jit(solution)/shard_map/reduce_scatter | solution.py:230
  1528.0 91.7 %reduce-scatter.5.cloned.1.call-start = ((), (), s32[]{:S(2)}) async-start(), calls=%async_computation.15 | async-start | bytes 5242880 | tf_op jit(solution)/shard_map/reduce_scatter | solution.py:233
  1528.7 176.4 %all-reduce.23.cloned.1.call-start = ((), (), s32[]{:S(2)}) async-start(), calls=%async_computation.19 | async-start | bytes 4980736 | tf_op jit(solution)/shard_map/psum | solution.py:255
  1633.3 299.6 %all-reduce.17.cloned.1.call-start = ((), (), s32[]{:S(2)}) async-start(), calls=%async_computation.16 | async-start | bytes 25165824 | tf_op jit(solution)/shard_map/psum | solution.py:14
  1645.8 59.4 %copy-start.71 = (f32[2,128]{1,0:T(2,128)S(1)}, f32[2,128]{1,0:T(2,128)}, u32[]{:S(2)}) copy-start(f32[2,128]{1,0:T(2,128)} %copy-done.70) | copy-start | bytes 3076
  1647.2 59.0 %copy-start.7 = (bf16[4,2,64,2048]{3,2,0,1:T(8,128)(2,1)S(1)}, bf16[4,2,64,2048]{3,2,0,1:T(8,128)(2,1)}, u32[]{:S(2)}) copy-start(bf16[4,2,64,2048]{3,2,0,1:T(8,128)(2,1)} %copy-done.6) | copy-start | bytes 6291460
  1709.6 747.2 %all-reduce.19.cloned.1.call-start = ((), (), s32[]{:S(2)}) async-start(), calls=%async_computation.17 | async-start | bytes 25165824 | tf_op jit(solution)/shard_map/psum | solution.py:13
  1938.0 109.0 %all-to-all-start.1 = ((bf16[2,256,2048]{2,0,1:T(2,128)(2,1)}), bf16[2,256,2048]{2,0,1:T(2,128)(2,1)S(1)}, u32[]{:S(2)}, u32[]{:S(2)}) async-start(bf16[2,256,2048]{2,0,1:T(2,128)(2,1)} %copy.68), calls=%async_computation.1 | async-start | bytes 4194304 | tf_op jit(solution)/shard_map/all_to_all | solution.py:283
  2047.0 102.1 %all-to-all-start.3 = ((bf16[2,256,2048]{2,0,1:T(2,128)(2,1)}), bf16[2,256,2048]{2,0,1:T(2,128)(2,1)}, u32[]{:S(2)}, u32[]{:S(2)}) async-start(bf16[2,256,2048]{2,0,1:T(2,128)(2,1)} %copy.76), calls=%async_computation.5 | async-start | bytes 4194304 | tf_op jit(solution)/shard_map/all_to_all | solution.py:284
  (76 other events, 261.3 us)
Sparse Core Ops, SparseCore 0:
  9.6 255.7 all-gather.6
  274.7 34.1 all-gather.10
  311.0 35.0 all-gather.8
  347.5 80.7 all-gather.12
  435.2 112.0 all-reduce.12
  548.8 286.7 all-gather.14
  837.2 284.9 all-gather.16
  1137.4 111.6 all-reduce.14
  1305.7 113.2 all-reduce.20
  1528.1 44.4 reduce-scatter.2
  1575.2 44.4 reduce-scatter.4
  1633.4 71.6 all-reduce.22
  1709.7 223.1 all-reduce.16
  1936.2 520.5 all-reduce.18
